TPU v7x, 32 devices: a whole 2x2x4 slice. The times are simulated.
32 devices in a mesh: seq: 8 (over z, y), tp: 4 (over x, core).
Axes of the slice: x: 2, y: 2, z: 4, core: 2. Of those that a mesh axis runs over, the one named last changes fastest.
Arguments:
- layer_activation: bfloat16 [3072, 2048], P('seq', 'tp'), may hold values from -6 to 6
- sequence_label: int32 [3072], P('seq'), may hold values from 0 to 2, as said below
- sequence_extents: int32 [2], replicated, may hold values from 1 to 1920, as said below
- destination_slots: int32 [2], replicated, may hold values from 0 to 7, as said below
- entry_layernorm_coef: float32 [2048], replicated, may hold values from 0.5 to 1.5
- lagged_blend_coefs: float32 [6, 2048], replicated, may hold values from 0 to 1
- query_matrix: bfloat16 [2048, 2048], P(None, 'tp'), may hold values from -0.125 to 0.125
- lookup_matrix: bfloat16 [2048, 2048], P(None, 'tp'), may hold values from -0.125 to 0.125
- content_matrix: bfloat16 [2048, 2048], P(None, 'tp'), may hold values from -0.125 to 0.125
- readout_matrix: bfloat16 [2048, 2048], P('tp'), may hold values from -0.125 to 0.125
- forgetting_narrow_matrix: bfloat16 [2048, 96], replicated, may hold values from -0.125 to 0.125
- forgetting_widen_matrix: bfloat16 [96, 2048], P(None, 'tp'), may hold values from -2.5 to 2.5
- forgetting_offset: float32 [2048], P('tp'), may hold values from -11 to -3.5
- stepsize_narrow_matrix: bfloat16 [2048, 96], replicated, may hold values from -0.125 to 0.125
- stepsize_widen_matrix: bfloat16 [96, 2048], P(None, 'tp'), may hold values from -0.625 to 0.625
- stepsize_offset: float32 [2048], P('tp'), may hold values from -4 to 4
- gating_narrow_matrix: bfloat16 [2048, 256], replicated, may hold values from -0.125 to 0.125
- gating_widen_matrix: bfloat16 [256, 2048], P(None, 'tp'), may hold values from -0.375 to 0.375
- erasure_lookup_coef: float32 [2048], P('tp'), may hold values from 0.5 to 1.5
- lookup_step_fraction: float32 [2048], P('tp'), may hold values from 0 to 1
- diagonal_reward_coef: float32 [2048], P('tp'), may hold values from -3 to 3
- group_layernorm_coef: float32 [2048], P('tp'), may hold values from 0.5 to 1.5
Outputs:
- mixed: bfloat16 [3072, 2048], P('seq', 'tp')
- final_states: float32 [8, 32, 64, 64], P('seq', 'tp')
- final_rows: bfloat16 [8, 2048], P('seq', 'tp')
Inputs may be any that keep to these rules, and one draw needn't show every extreme that they name: `sequence_label`: token p is in prompt 0 for p < sequence_extents[0], in prompt 1 for the next sequence_extents[1] tokens, and padding (2) after them; at least one padding token. `sequence_extents`: one length is exactly 1920, the other at least 768; their sum is under 3072. `destination_slots`: the two owners differ, and one of them is the last index of seq.
All inputs are finite; a program needn't handle non-finite values.
Results may differ from a plain program's by a relative error of at most 0.012.
Values may be sent and summed in bfloat16 or wider, within the bound.
A program may use at most 128 MiB of HBM per device.

v0:
```python
import jax
import jax.numpy as jnp
from jax import lax
from jax.sharding import PartitionSpec as P

CHANNELS_PER_ONE = 64
PROMPTS = 2
EPS = 1e-05
GROUP_EPS = 0.00064


def from_behind(array, axis, by):
    length = lax.axis_size(axis)
    pairs = [(i, i + by) for i in range(length) if 0 <= i + by < length]
    return lax.ppermute(array, axis, pairs)


def broadcast(value, axis, source):
    kept = jnp.where(lax.axis_index(axis) == source, value, 0).astype(value.dtype)
    return lax.psum(kept, axis)


def matmul(left, right):
    return jnp.dot(left, right, preferred_element_type=jnp.float32)


def compose(earlier_map, later_map):
    return jnp.einsum("hij,hjk->hik", earlier_map, later_map, precision=lax.Precision.HIGHEST)


def on_device(
    layer_activation,
    sequence_label,
    sequence_extents,
    destination_slots,
    entry_layernorm_coef,
    lagged_blend_coefs,
    query_matrix,
    lookup_matrix,
    content_matrix,
    readout_matrix,
    forgetting_narrow_matrix,
    forgetting_widen_matrix,
    forgetting_offset,
    stepsize_narrow_matrix,
    stepsize_widen_matrix,
    stepsize_offset,
    gating_narrow_matrix,
    gating_widen_matrix,
    erasure_lookup_coef,
    lookup_step_fraction,
    diagonal_reward_coef,
    group_layernorm_coef,
):
    highest = lax.Precision.HIGHEST
    segment_length = layer_activation.shape[0]
    stepsize_fraction = query_matrix.shape[1]
    local_attentioners = stepsize_fraction // CHANNELS_PER_ONE
    position = lax.axis_index("seq")
    column = lax.axis_index("tp")
    gathered = lax.all_gather(layer_activation, "tp", axis=1, tiled=True)
    floats = gathered.astype(jnp.float32)
    average = jnp.mean(floats, axis=1, keepdims=True)
    centred = floats - average
    variance = jnp.mean(centred * centred, axis=1, keepdims=True)
    normed = (centred * lax.rsqrt(variance + EPS) * entry_layernorm_coef).astype(jnp.bfloat16)
    normal_f = normed.astype(jnp.float32)
    arrived = from_behind(normed[-1:], "seq", 1)
    bounds = jnp.cumsum(sequence_extents)
    first_token = position * segment_length
    before = first_token - 1
    segment_before = (before >= bounds[0]).astype(jnp.int32) + (before >= bounds[1]).astype(
        jnp.int32
    )
    joined = (segment_before == sequence_label[0]) & (position > 0)
    continues = jnp.concatenate([joined[None], sequence_label[1:] == sequence_label[:-1]])
    previous = jnp.concatenate([arrived.astype(jnp.float32), normal_f[:-1]], axis=0)
    previous = jnp.where(continues[:, None], previous, jnp.zeros_like(previous))
    difference = previous - normal_f

    def blended(which):
        return (normal_f + difference * lagged_blend_coefs[which]).astype(jnp.bfloat16)

    receptance = matmul(blended(0), query_matrix)
    keys = matmul(blended(2), lookup_matrix)
    values = matmul(blended(3), content_matrix)
    decay_hidden = jnp.tanh(matmul(blended(1), forgetting_narrow_matrix)).astype(jnp.bfloat16)
    learn_hidden = matmul(blended(4), stepsize_narrow_matrix).astype(jnp.bfloat16)
    gate_hidden = jax.nn.sigmoid(matmul(blended(5), gating_narrow_matrix)).astype(jnp.bfloat16)
    log_rate = (
        -jax.nn.softplus(-(forgetting_offset + matmul(decay_hidden, forgetting_widen_matrix))) - 0.5
    )
    log_decay = -jnp.exp(log_rate)
    learning = jax.nn.sigmoid(stepsize_offset + matmul(learn_hidden, stepsize_widen_matrix))
    gating_signal = matmul(gate_hidden, gating_widen_matrix)
    removal = (keys * erasure_lookup_coef).reshape(
        segment_length, local_attentioners, CHANNELS_PER_ONE
    )
    removal = removal * lax.rsqrt(jnp.sum(removal * removal, axis=-1, keepdims=True) + 1e-06)
    written = keys * (1.0 + (learning - 1.0) * lookup_step_fraction)
    split_queries = receptance.reshape(segment_length, local_attentioners, CHANNELS_PER_ONE)
    split_lookups = written.reshape(segment_length, local_attentioners, CHANNELS_PER_ONE)
    split_contents = values.reshape(segment_length, local_attentioners, CHANNELS_PER_ONE)
    head_w = log_decay.reshape(segment_length, local_attentioners, CHANNELS_PER_ONE)
    head_a = learning.reshape(segment_length, local_attentioners, CHANNELS_PER_ONE)
    padded_v = jnp.concatenate([split_contents, jnp.zeros_like(split_contents)], axis=-1)
    local_ends = bounds - 1 - first_token
    block_len = min(64, segment_length)
    blocks = segment_length // block_len
    steps_in = jnp.arange(block_len, dtype=jnp.int32)
    strict_lower = steps_in[:, None] > steps_in[None, :]
    with_diag = steps_in[:, None] >= steps_in[None, :]
    unit_eye = jnp.eye(block_len, dtype=jnp.float32)

    def regroup(array):
        return array.reshape((blocks, block_len) + array.shape[1:])

    def block_step(carry, inputs):
        stacked, saved = carry
        block_start, still, r_blk, k_blk, v_blk, n_blk, lw_blk, a_blk = inputs
        restarts = jnp.logical_not(still).astype(jnp.int32)
        epochs = jnp.cumsum(restarts)
        from_start = (epochs == 0).astype(jnp.float32)
        log_total = jnp.cumsum(lw_blk, axis=0)
        query_a = -n_blk * jnp.exp(log_total - lw_blk)
        scaled_beta = n_blk * a_blk * jnp.exp(-log_total)
        scaled_key = k_blk * jnp.exp(-log_total)
        scaled_query = r_blk * jnp.exp(log_total)
        same_run = epochs[:, None] == epochs[None, :]
        strict_mask = (strict_lower & same_run).astype(jnp.float32)
        diag_mask = (with_diag & same_run).astype(jnp.float32)

        def paired(left, right, mask):
            return jnp.einsum("thj,shj->hts", left, right, precision=highest) * mask[None]

        mix_beta = paired(query_a, scaled_beta, strict_mask)
        mix_key = paired(query_a, scaled_key, strict_mask)
        read_beta = paired(scaled_query, scaled_beta, diag_mask)
        read_key = paired(scaled_query, scaled_key, diag_mask)
        from_state = jnp.einsum(
            "thj,hij->hti", query_a * from_start[:, None, None], stacked, precision=highest
        )
        right_side = from_state + jnp.einsum("hts,shi->hti", mix_key, v_blk, precision=highest)
        pseudo = jax.scipy.linalg.solve_triangular(
            unit_eye[None] - mix_beta, right_side, lower=True, unit_diagonal=True
        )
        outputs_blk = jnp.einsum(
            "thj,hij->thi", scaled_query * from_start[:, None, None], stacked, precision=highest
        )
        outputs_blk = outputs_blk + jnp.einsum("hts,hsi->thi", read_beta, pseudo, precision=highest)
        outputs_blk = outputs_blk + jnp.einsum("hts,shi->thi", read_key, v_blk, precision=highest)

        def state_at(moment):
            growth = jnp.exp(lax.dynamic_index_in_dim(log_total, moment, 0, keepdims=False))
            epoch_now = lax.dynamic_index_in_dim(epochs, moment, 0, keepdims=False)
            chosen = ((steps_in <= moment) & (epochs == epoch_now)).astype(jnp.float32)
            weight_beta = scaled_beta * chosen[:, None, None] * growth[None]
            weight_key = scaled_key * chosen[:, None, None] * growth[None]
            start_part = stacked * (growth * (epoch_now == 0).astype(jnp.float32))[:, None, :]
            result = start_part + jnp.einsum("hsi,shj->hij", pseudo, weight_beta, precision=highest)
            return result + jnp.einsum("shi,shj->hij", v_blk, weight_key, precision=highest)

        new_stacked = state_at(jnp.int32(block_len - 1))
        updated = []
        for prompt in range(PROMPTS):
            offset_end = local_ends[prompt] - block_start
            inside = (offset_end >= 0) & (offset_end < block_len)
            moment = jnp.clip(offset_end, 0, block_len - 1)
            updated.append(jnp.where(inside, state_at(moment), saved[prompt]))
        return ((new_stacked, jnp.stack(updated)), outputs_blk)

    identity = jnp.broadcast_to(
        jnp.eye(CHANNELS_PER_ONE, dtype=jnp.float32),
        (local_attentioners, CHANNELS_PER_ONE, CHANNELS_PER_ONE),
    )
    start_stack = jnp.concatenate([jnp.zeros_like(identity), identity], axis=1)
    start_saved = jnp.zeros(
        (PROMPTS, local_attentioners, 2 * CHANNELS_PER_ONE, CHANNELS_PER_ONE), jnp.float32
    )
    block_starts = jnp.arange(blocks, dtype=jnp.int32) * block_len
    scan_inputs = (
        block_starts,
        regroup(continues),
        regroup(split_queries),
        regroup(split_lookups),
        regroup(padded_v),
        regroup(removal),
        regroup(head_w),
        regroup(head_a),
    )
    (final_stack, saved), grouped_out = lax.scan(
        block_step, (start_stack, start_saved), scan_inputs
    )
    outputs = grouped_out.reshape(segment_length, local_attentioners, 2 * CHANNELS_PER_ONE)
    local_state = final_stack[:, :CHANNELS_PER_ONE]
    transition = final_stack[:, CHANNELS_PER_ONE:]

    def passing(turn, incoming):
        return from_behind(
            (compose(incoming, transition) + local_state).astype(jnp.bfloat16), "seq", 1
        ).astype(jnp.float32)

    state_in = lax.fori_loop(0, lax.axis_size("seq") - 1, passing, jnp.zeros_like(local_state))
    readout = outputs[:, :, :CHANNELS_PER_ONE] + jnp.einsum(
        "hij,thj->thi", state_in, outputs[:, :, CHANNELS_PER_ONE:], precision=highest
    )
    centre = readout - jnp.mean(readout, axis=-1, keepdims=True)
    spread = jnp.mean(centre * centre, axis=-1, keepdims=True)
    group_standardized = (
        centre
        * lax.rsqrt(spread + GROUP_EPS)
        * group_layernorm_coef.reshape(local_attentioners, CHANNELS_PER_ONE)
    )
    diagonal_reward = (
        jnp.sum(
            split_queries
            * split_lookups
            * diagonal_reward_coef.reshape(local_attentioners, CHANNELS_PER_ONE),
            axis=-1,
            keepdims=True,
        )
        * split_contents
    )
    visible_entries = (
        (group_standardized + diagonal_reward).reshape(segment_length, stepsize_fraction)
        * gating_signal
    ).astype(jnp.bfloat16)
    partial_value = matmul(visible_entries, readout_matrix)
    summed = lax.psum_scatter(
        partial_value.astype(jnp.bfloat16), "tp", scatter_dimension=1, tiled=True
    ).astype(jnp.float32)
    mixed = (summed + layer_activation.astype(jnp.float32)).astype(jnp.bfloat16)
    final_states = jnp.zeros(
        (1, local_attentioners, CHANNELS_PER_ONE, CHANNELS_PER_ONE), jnp.float32
    )
    final_rows = jnp.zeros((1, stepsize_fraction), jnp.bfloat16)
    for prompt in range(PROMPTS):
        last_token = bounds[prompt] - 1
        holder = last_token // segment_length
        inside = jnp.clip(last_token - first_token, 0, segment_length - 1)
        recorded = saved[prompt]
        state_end = (
            compose(state_in, recorded[:, CHANNELS_PER_ONE:]) + recorded[:, :CHANNELS_PER_ONE]
        )
        row_end = lax.dynamic_slice(
            normal_f, (inside, column * stepsize_fraction), (1, stepsize_fraction)
        )
        got_state, got_row = (
            broadcast(state_end.astype(jnp.bfloat16), "seq", holder).astype(state_end.dtype),
            broadcast(row_end.astype(jnp.bfloat16), "seq", holder).astype(row_end.dtype),
        )
        is_owner = position == destination_slots[prompt]
        final_states = jnp.where(is_owner, got_state[None], final_states)
        final_rows = jnp.where(is_owner, got_row.astype(jnp.bfloat16), final_rows)
    return (mixed, final_states, final_rows)


def solution(mesh):
    return jax.shard_map(
        on_device,
        mesh=mesh,
        in_specs=(
            P("seq", "tp"),
            P("seq"),
            P(),
            P(),
            P(),
            P(),
            P(None, "tp"),
            P(None, "tp"),
            P(None, "tp"),
            P("tp", None),
            P(),
            P(None, "tp"),
            P("tp"),
            P(),
            P(None, "tp"),
            P("tp"),
            P(),
            P(None, "tp"),
            P("tp"),
            P("tp"),
            P("tp"),
            P("tp"),
        ),
        out_specs=(P("seq", "tp"), P("seq", "tp", None, None), P("seq", "tp")),
        check_vma=False,
    )
```

profile of v0, /device:TPU:0, one launch (start us, length us, event | category | flops | bytes accessed | tf_op | source)
XLA Modules:
  0.0 698.0 jit_solution(5239069506846674704)
XLA Ops:
  14.6 17.4 %all-gather.2.cloned.1.call-done = bf16[384,2048]{1,0:T(8,128)(2,1)} async-done(((bf16[384,512]{1,0:T(8,128)(2,1)}), bf16[384,2048]{1,0:T(8,128)(2,1)}) %all-gather.2.cloned.1.call-update) | async-done | bytes 1572880 | tf_op jit(solution)/shard_map/all_gather | solution.py:61
  37.5 3.4 collective-permute-start.1
  42.8 3.5 slice.133
  46.3 3.9 fusion.101
  51.7 5.1 fusion.72
  56.7 2.5 reshape_reshape.15
  59.3 5.5 fusion.149
  68.7 5.1 fusion.139
  73.8 2.7 reshape_reshape.12
  76.5 2.6 reshape.279
  80.6 4.5 fusion.74
  86.8 2.8 concatenate.15.clone
  92.1 414.9 %while.27 = (s32[]{:T(128)}, f32[8,128,64]{1,2,0:T(8,128)S(1)}, f32[2,8,128,64]{2,3,1,0:T(8,128)}, f32[6,64,8,128]{3,2,1,0:T(8,128)}, f32[6,64,8,64]{3,2,1,0:T(8...) while((s32[]{:T(128)}, f32[8,128,64]{1,2,0:T(8,128)S(1)}, ...), condition=%wide.region_7.8_spmd.clone.clone, body=%wide.region_4.7_spmd.clone.clone.sunk | while | flops 708762112 | bytes 20262212 | solution.py:191
  103.1 2.4 multiply_multiply_fusion.8
  108.9 40.7 %custom-call.9 = f32[8,1,64,64]{2,3,1,0:T(8,128)} custom-call(f32[8,1,64,64]{3,2,1,0:T(8,128)} %fusion.259), custom_call_target="InvertDiagBlocksLowerTriangular" | custom-call | tf_op jit(solution)/shard_map/while/body/eval_jaxpr/jit(_solve_triangular)/vmap()/triangular_solve | solution.py:144
  172.3 2.4 multiply_multiply_fusion.8
  178.1 40.7 %custom-call.9 = f32[8,1,64,64]{2,3,1,0:T(8,128)} custom-call(f32[8,1,64,64]{3,2,1,0:T(8,128)} %fusion.259), custom_call_target="InvertDiagBlocksLowerTriangular" | custom-call | tf_op jit(solution)/shard_map/while/body/eval_jaxpr/jit(_solve_triangular)/vmap()/triangular_solve | solution.py:144
  241.4 2.4 multiply_multiply_fusion.8
  247.2 40.7 %custom-call.9 = f32[8,1,64,64]{2,3,1,0:T(8,128)} custom-call(f32[8,1,64,64]{3,2,1,0:T(8,128)} %fusion.259), custom_call_target="InvertDiagBlocksLowerTriangular" | custom-call | tf_op jit(solution)/shard_map/while/body/eval_jaxpr/jit(_solve_triangular)/vmap()/triangular_solve | solution.py:144
  310.6 2.4 multiply_multiply_fusion.8
  316.4 40.7 %custom-call.9 = f32[8,1,64,64]{2,3,1,0:T(8,128)} custom-call(f32[8,1,64,64]{3,2,1,0:T(8,128)} %fusion.259), custom_call_target="InvertDiagBlocksLowerTriangular" | custom-call | tf_op jit(solution)/shard_map/while/body/eval_jaxpr/jit(_solve_triangular)/vmap()/triangular_solve | solution.py:144
  385.5 40.7 %custom-call.9 = f32[8,1,64,64]{2,3,1,0:T(8,128)} custom-call(f32[8,1,64,64]{3,2,1,0:T(8,128)} %fusion.259), custom_call_target="InvertDiagBlocksLowerTriangular" | custom-call | tf_op jit(solution)/shard_map/while/body/eval_jaxpr/jit(_solve_triangular)/vmap()/triangular_solve | solution.py:144
  448.9 2.4 multiply_multiply_fusion.8
  454.7 40.7 %custom-call.9 = f32[8,1,64,64]{2,3,1,0:T(8,128)} custom-call(f32[8,1,64,64]{3,2,1,0:T(8,128)} %fusion.259), custom_call_target="InvertDiagBlocksLowerTriangular" | custom-call | tf_op jit(solution)/shard_map/while/body/eval_jaxpr/jit(_solve_triangular)/vmap()/triangular_solve | solution.py:144
  507.3 2.4 copy.127
  509.7 2.4 slice_bitcast_fusion.1
  514.2 2.8 copy.135
  517.1 55.1 %while.28 = (s32[]{:T(128)}, f32[8,64,64]{2,1,0:T(8,128)S(1)}, f32[8,64,64]{2,1,0:T(8,128)S(1)}, f32[8,64,64]{2,1,0:T(8,128)S(1)}, s32[]{:T(128)}, /*index=5*/s32[]{:T(128)}) while((s32[]{:T(128)}, f32[8,64,64]{2,1,0:T(8,128)S(1)}, f32[8,64,64]{2,1,0:T(8,128)S(1)}, f32[8,64,64]{2,1,0:T(8,128)S(1)}, s32[]{:T(128)}, ...), condition=%wide.region_9.10_spmd.clone, body=%wide.region_8.9_spmd.clone.sunk | while | flops 25296900 | bytes 917623 | solution.py:203
  517.4 3.4 collective-permute-start
  520.8 2.8 collective-permute-done
  524.1 4.4 collective-permute-start
  528.5 2.5 collective-permute-done
  531.4 4.4 collective-permute-start
  535.8 2.5 collective-permute-done
  538.7 5.2 collective-permute-start
  543.9 2.5 collective-permute-done
  546.9 5.3 collective-permute-start
  552.1 2.5 collective-permute-done
  555.1 5.3 collective-permute-start
  560.3 3.0 collective-permute-done
  563.8 5.6 collective-permute-start
  569.4 2.5 collective-permute-done
  572.1 4.1 fusion.157
  579.0 4.4 fusion.116
  585.6 4.1 convolution_convert_fusion
  592.5 22.7 %all-reduce.2 = (bf16[1,512]{1,0:T(2,128)(2,1)S(1)}, bf16[1,512]{1,0:T(2,128)(2,1)S(1)}) all-reduce(bf16[1,512]{1,0:T(2,128)(2,1)S(1)} %get-tuple-element.333, bf16[1,512]{1,0:T(2,128)(2,1)S(1)} %get-tuple-element.332), channel_id=1, replica_groups=mesh['seq'=8,'tp'=4] {'seq'}, use_global_device_ids=true, to_apply=%region_16.17 | all-reduce | flops 1024 | bytes 4096 | tf_op jit(solution)/shard_map/psum | solution.py:20
  615.9 43.6 %all-reduce.6.cloned.1.call-done = (bf16[8,64,64]{2,1,0:T(8,128)(2,1)}, bf16[8,64,64]{2,1,0:T(8,128)(2,1)}) async-done(((bf16[8,64,64]{2,1,0:T(8,128)(2,1)}, bf16[8,64,64]{2,1,0:T(8,128)(2,1)}), (bf16[8,64,64]{2,1,0:T(8,128)(2,1)}, bf16[8,64,64]{2,1,0:T(8,128)(2,1)})) %all-reduce.6.cloned.1.call-update) | async-done | bytes 131088 | tf_op jit(solution)/shard_map/psum | solution.py:20
  661.1 28.5 %reduce-scatter.2.cloned.1.call-done = bf16[384,512]{1,0:T(8,128)(2,1)} async-done(((bf16[384,2048]{1,0:T(8,128)(2,1)}), bf16[384,512]{1,0:T(8,128)(2,1)}) %reduce-scatter.2.cloned.1.call-update) | async-done | bytes 393232 | tf_op jit(solution)/shard_map/reduce_scatter | solution.py:229
  (336 shorter events, 168.1 us)
Async XLA Ops:
  7.2 52.1 %copy-start = (bf16[2048,512]{1,0:T(8,128)(2,1)S(1)}, bf16[2048,512]{1,0:T(8,128)(2,1)}, u32[]{:S(2)}) copy-start(bf16[2048,512]{1,0:T(8,128)(2,1)} %param.33) | copy-start | bytes 6291460
  7.2 28.6 %copy-start.15 = (f32[2048]{0:T(1024)S(1)}, f32[2048]{0:T(1024)}, u32[]{:S(2)}) copy-start(f32[2048]{0:T(1024)} %param.30) | copy-start | bytes 24580
  7.2 24.8 %all-gather.2.cloned.1.call-start = ((), (), s32[]{:S(2)}) async-start(), calls=%async_computation.1 | async-start | bytes 1966080 | tf_op jit(solution)/shard_map/all_gather | solution.py:61
  7.9 651.5 %all-reduce.6.cloned.1.call-start = ((), (), s32[]{:S(2)}) async-start(), calls=%async_computation.3 | async-start | bytes 524288 | tf_op jit(solution)/shard_map/psum | solution.py:20
  14.6 27.9 %copy-start.16 = (f32[512]{0:T(512)S(1)}, f32[512]{0:T(512)}, u32[]{:S(2)}) copy-start(f32[512]{0:T(512)} %param.46) | copy-start | bytes 6148
  14.6 28.0 %copy-start.17 = (f32[512]{0:T(512)S(1)}, f32[512]{0:T(512)}, u32[]{:S(2)}) copy-start(f32[512]{0:T(512)} %param.47) | copy-start | bytes 6148
  32.0 3.8 copy-start.5
  36.3 1.2 copy-start.4
  37.5 8.7 %collective-permute-start.1 = (bf16[1,2048]{1,0:T(2,128)(2,1)S(1)}, bf16[1,2048]{1,0:T(2,128)(2,1)S(1)}, u32[]{:S(2)}, u32[]{:S(2)}) collective-permute-start(bf16[1,2048]{1,0:T(2,128)(2,1)S(1)} %slice.132), channel_id=1, source_target_pairs={{0,4},{4,8},{8,12},{12,16},{16,20},{20,24},{24,28},{1,5},{5,9},{9,... | collective-permute-start | bytes 12296 | tf_op jit(solution)/shard_map/ppermute | solution.py:15
  42.8 3.5 copy-start.19
  42.8 3.5 copy-start.20
  51.7 7.6 %copy-start.21 = (f32[512]{0:T(512)S(1)}, f32[512]{0:T(512)}, u32[]{:S(2)}) copy-start(f32[512]{0:T(512)} %param.44) | copy-start | bytes 6148
  51.7 7.6 %copy-start.22 = (f32[512]{0:T(512)S(1)}, f32[512]{0:T(512)}, u32[]{:S(2)}) copy-start(f32[512]{0:T(512)} %param.45) | copy-start | bytes 6148
  64.8 3.9 copy-start.23
  73.8 5.3 copy-start.14
  85.1 6.1 copy-start.9
  86.8 2.8 copy-start.7
  149.6 4.9 copy-start.1
  155.5 2.8 copy-start.2
  218.7 4.9 copy-start.1
  224.6 2.8 copy-start.2
  287.9 4.9 copy-start.1
  293.8 2.8 copy-start.2
  357.1 4.9 copy-start.1
  363.0 2.8 copy-start.2
  426.2 4.9 copy-start.1
  432.1 2.8 copy-start.2
  495.4 4.9 copy-start.1
  501.3 2.8 copy-start.2
  509.7 2.4 copy-start.6
  512.1 4.9 copy-start.3
  517.4 6.2 collective-permute-start
  524.1 6.9 collective-permute-start
  531.4 6.9 collective-permute-start
  538.7 7.7 %collective-permute-start = (bf16[8,64,64]{2,1,0:T(8,128)(2,1)S(1)}, bf16[8,64,64]{2,1,0:T(8,128)(2,1)S(1)}, u32[]{:S(2)}, u32[]{:S(2)}) collective-permute-start(bf16[8,64,64]{2,1,0:T(8,128)(2,1)S(1)} %fusion.267), channel_id=1, source_target_pairs={{0,4},{4,8},{8,12},{12,16},{16,20},{20,24},{24,28},{1,5},{5,9},{9,... | collective-permute-start | bytes 196616 | tf_op jit(solution)/shard_map/while/body/eval_jaxpr/ppermute | solution.py:15
  546.9 7.8 %collective-permute-start = (bf16[8,64,64]{2,1,0:T(8,128)(2,1)S(1)}, bf16[8,64,64]{2,1,0:T(8,128)(2,1)S(1)}, u32[]{:S(2)}, u32[]{:S(2)}) collective-permute-start(bf16[8,64,64]{2,1,0:T(8,128)(2,1)S(1)} %fusion.267), channel_id=1, source_target_pairs={{0,4},{4,8},{8,12},{12,16},{16,20},{20,24},{24,28},{1,5},{5,9},{9,... | collective-permute-start | bytes 196616 | tf_op jit(solution)/shard_map/while/body/eval_jaxpr/ppermute | solution.py:15
  555.1 8.3 %collective-permute-start = (bf16[8,64,64]{2,1,0:T(8,128)(2,1)S(1)}, bf16[8,64,64]{2,1,0:T(8,128)(2,1)S(1)}, u32[]{:S(2)}, u32[]{:S(2)}) collective-permute-start(bf16[8,64,64]{2,1,0:T(8,128)(2,1)S(1)} %fusion.267), channel_id=1, source_target_pairs={{0,4},{4,8},{8,12},{12,16},{16,20},{20,24},{24,28},{1,5},{5,9},{9,... | collective-permute-start | bytes 196616 | tf_op jit(solution)/shard_map/while/body/eval_jaxpr/ppermute | solution.py:15
  563.8 8.1 %collective-permute-start = (bf16[8,64,64]{2,1,0:T(8,128)(2,1)S(1)}, bf16[8,64,64]{2,1,0:T(8,128)(2,1)S(1)}, u32[]{:S(2)}, u32[]{:S(2)}) collective-permute-start(bf16[8,64,64]{2,1,0:T(8,128)(2,1)S(1)} %fusion.267), channel_id=1, source_target_pairs={{0,4},{4,8},{8,12},{12,16},{16,20},{20,24},{24,28},{1,5},{5,9},{9,... | collective-permute-start | bytes 196616 | tf_op jit(solution)/shard_map/while/body/eval_jaxpr/ppermute | solution.py:15
  572.1 4.3 copy-start.8
  572.1 4.3 copy-start.10
  579.0 4.4 copy-start.13
  579.0 5.5 copy-start.12
  585.6 4.2 copy-start.18
  585.6 104.1 %copy-start.11 = (bf16[384,512]{1,0:T(8,128)(2,1)S(1)}, bf16[384,512]{1,0:T(8,128)(2,1)}, u32[]{:S(2)}) copy-start(bf16[384,512]{1,0:T(8,128)(2,1)} %param.26) | copy-start | bytes 1179652
  585.6 104.0 %reduce-scatter.2.cloned.1.call-start = ((), (), s32[]{:S(2)}) async-start(), calls=%async_computation.2 | async-start | bytes 1966080 | tf_op jit(solution)/shard_map/reduce_scatter | solution.py:229
Sparse Core Ops, SparseCore 0:
  9.6 22.3 all-gather.1
  585.7 73.6 all-reduce.5
  662.1 27.4 reduce-scatter.1
where the time goes:
time: 701 us; the launch traced here: 698 us
  other arithmetic  299 us (43%)
  matrix products  120 us (17%)
  waiting for transfers between devices  109 us (16%)
  local copies, waits for them, and re-layouts  62.6 us (9%)
  starting transfers between devices  36.9 us (5%)
  loops' own time  29.5 us (4%)
  blocking collectives  22.7 us (3%)
  between operations  18.8 us (3%)
    another operation x18, other arithmetic, block_step(): jax.scipy.linalg.solve_triangular(unit_eye[None] - mix_beta, right_side,...  245 us
    psum x1, waiting for transfers between devices, broadcast(): return lax.psum(kept, axis)  43.6 us
    ppermute x8, starting transfers between devices, from_behind(): return lax.ppermute(array, axis, pairs)  36.8 us
    dot_general x7, matrix products, matmul(): return jnp.dot(left, right, preferred_element_type=jnp.float32)  32.6 us
    another operation x1, loops' own time, on_device(): lax.scan(block_step, (start_stack, start_saved), scan_inputs)  29.1 us
    reduce_scatter x1, waiting for transfers between devices, on_device(): lax.psum_scatter(partial_value.astype(jnp.bfloat16), 'tp', scatter_dimens...  28.5 us
    psum x1, blocking collectives, broadcast(): return lax.psum(kept, axis)  22.7 us
    dot_general x24, matrix products, paired(): jnp.einsum('thj,shj->hts', left, right, precision=highest) * mask[None]  18.6 us
  transfers between devices with their start and end apart: 11, of which 10 were waited for; matrix products, arithmetic and copies ran while one was open for 2% of the time, Pallas kernels for 0%

commit v1 on v0

--- a/solution.py
+++ b/solution.py
@@ -58,7 +58,26 @@
     local_attentioners = stepsize_fraction // CHANNELS_PER_ONE
     position = lax.axis_index("seq")
     column = lax.axis_index("tp")
-    gathered = lax.all_gather(layer_activation, "tp", axis=1, tiled=True)
+    devices, index, rows = (lax.axis_size("tp"), lax.axis_index("tp"), layer_activation.shape[1])
+    upward = [(i_2, (i_2 + 1) % devices) for i_2 in range(devices)]
+    backward = [(i_2, (i_2 - 1) % devices) for i_2 in range(devices)]
+    gathered = jnp.zeros(
+        (*layer_activation.shape[:1], devices * rows, *layer_activation.shape[1 + 1 :]),
+        layer_activation.dtype,
+    )
+    gathered = lax.dynamic_update_slice_in_dim(gathered, layer_activation, index * rows, axis=1)
+    from_left = from_right = layer_activation
+    middle = devices // 2
+    for step in range(1, middle + 1):
+        from_left = lax.ppermute(from_left, "tp", upward)
+        gathered = lax.dynamic_update_slice_in_dim(
+            gathered, from_left, (index - step) % devices * rows, axis=1
+        )
+        if step < devices - middle:
+            from_right = lax.ppermute(from_right, "tp", backward)
+            gathered = lax.dynamic_update_slice_in_dim(
+                gathered, from_right, (index + step) % devices * rows, axis=1
+            )
     floats = gathered.astype(jnp.float32)
     average = jnp.mean(floats, axis=1, keepdims=True)
     centred = floats - average

time: 701 us -> 669 us (0.954)
  waiting for transfers between devices: 109 us -> 69.2 us
    reduce_scatter x1, waiting for transfers between devices: 28.5 us -> 0.01 us  [on_device(): lax.psum_scatter(partial_value.astype(jnp.bfloat16), 'tp', scatter_dimens...]
    all_gather x1 -> x0, waiting for transfers between devices: 17.4 us -> none  [on_device(): gathered = lax.all_gather(layer_activation, 'tp', axis=1, tiled=True)]
  transfers between devices with their start and end apart: 11 -> 13, of which waited for: 10 -> 10; matrix products, arithmetic and copies ran while one was open for 2% -> 2% of each run, Pallas kernels for 0% -> 0%
where the time goes in v1:
time: 669 us; the launch traced here: 666 us
  other arithmetic  296 us (44%)
  matrix products  120 us (18%)
  waiting for transfers between devices  69.2 us (10%)
  local copies, waits for them, and re-layouts  64.5 us (10%)
  starting transfers between devices  43.9 us (7%)
  loops' own time  28.8 us (4%)
  blocking collectives  23 us (3%)
  between operations  20.6 us (3%)
    another operation x18, other arithmetic, block_step(): jax.scipy.linalg.solve_triangular(unit_eye[None] - mix_beta, right_side,...  245 us
    psum x1, waiting for transfers between devices, broadcast(): return lax.psum(kept, axis)  45.8 us
    ppermute x8, starting transfers between devices, from_behind(): return lax.ppermute(array, axis, pairs)  38.8 us
    dot_general x7, matrix products, matmul(): return jnp.dot(left, right, preferred_element_type=jnp.float32)  32.5 us
    another operation x1, loops' own time, on_device(): lax.scan(block_step, (start_stack, start_saved), scan_inputs)  28.3 us
    psum x1, blocking collectives, broadcast(): return lax.psum(kept, axis)  23 us
    dot_general x24, matrix products, paired(): jnp.einsum('thj,shj->hts', left, right, precision=highest) * mask[None]  18.6 us
    ppermute x8, waiting for transfers between devices, from_behind(): return lax.ppermute(array, axis, pairs)  18.4 us
  transfers between devices with their start and end apart: 13, of which 10 were waited for; matrix products, arithmetic and copies ran while one was open for 2% of the time, Pallas kernels for 0%

profile of v1, /device:TPU:0, one launch (start us, length us, event | category | flops | bytes accessed | tf_op | source)
XLA Modules:
  0.0 665.9 jit_solution(1374590591658182451)
XLA Ops:
  14.0 3.8 collective-permute-done.1
  17.7 2.6 collective-permute-start.3
  28.7 5.2 collective-permute-start.4
  35.8 3.5 slice.133
  39.3 3.9 fusion.101
  44.7 5.0 fusion.72
  49.7 2.6 reshape_reshape.15
  52.3 5.5 fusion.149
  61.7 5.1 fusion.139
  66.9 2.7 reshape_reshape.12
  69.6 2.6 reshape.279
  73.6 4.5 fusion.74
  79.8 2.8 concatenate.15.clone
  85.1 413.9 %while.27 = (s32[]{:T(128)}, f32[8,128,64]{1,2,0:T(8,128)S(1)}, f32[2,8,128,64]{2,3,1,0:T(8,128)}, f32[6,64,8,128]{3,2,1,0:T(8,128)}, f32[6,64,8,64]{3,2,1,0:T(8...) while((s32[]{:T(128)}, f32[8,128,64]{1,2,0:T(8,128)S(1)}, ...), condition=%wide.region_7.8_spmd.clone.clone, body=%wide.region_4.7_spmd.clone.clone.sunk | while | flops 708762112 | bytes 20262212 | solution.py:210
  96.0 2.4 multiply_multiply_fusion.8
  101.8 40.7 %custom-call.9 = f32[8,1,64,64]{2,3,1,0:T(8,128)} custom-call(f32[8,1,64,64]{3,2,1,0:T(8,128)} %fusion.259), custom_call_target="InvertDiagBlocksLowerTriangular" | custom-call | tf_op jit(solution)/shard_map/while/body/eval_jaxpr/jit(_solve_triangular)/vmap()/triangular_solve | solution.py:163
  164.9 2.4 multiply_multiply_fusion.8
  170.7 40.7 %custom-call.9 = f32[8,1,64,64]{2,3,1,0:T(8,128)} custom-call(f32[8,1,64,64]{3,2,1,0:T(8,128)} %fusion.259), custom_call_target="InvertDiagBlocksLowerTriangular" | custom-call | tf_op jit(solution)/shard_map/while/body/eval_jaxpr/jit(_solve_triangular)/vmap()/triangular_solve | solution.py:163
  233.9 2.4 multiply_multiply_fusion.8
  239.7 40.7 %custom-call.9 = f32[8,1,64,64]{2,3,1,0:T(8,128)} custom-call(f32[8,1,64,64]{3,2,1,0:T(8,128)} %fusion.259), custom_call_target="InvertDiagBlocksLowerTriangular" | custom-call | tf_op jit(solution)/shard_map/while/body/eval_jaxpr/jit(_solve_triangular)/vmap()/triangular_solve | solution.py:163
  302.9 2.4 multiply_multiply_fusion.8
  308.7 40.7 %custom-call.9 = f32[8,1,64,64]{2,3,1,0:T(8,128)} custom-call(f32[8,1,64,64]{3,2,1,0:T(8,128)} %fusion.259), custom_call_target="InvertDiagBlocksLowerTriangular" | custom-call | tf_op jit(solution)/shard_map/while/body/eval_jaxpr/jit(_solve_triangular)/vmap()/triangular_solve | solution.py:163
  371.9 2.4 multiply_multiply_fusion.8
  377.7 40.7 %custom-call.9 = f32[8,1,64,64]{2,3,1,0:T(8,128)} custom-call(f32[8,1,64,64]{3,2,1,0:T(8,128)} %fusion.259), custom_call_target="InvertDiagBlocksLowerTriangular" | custom-call | tf_op jit(solution)/shard_map/while/body/eval_jaxpr/jit(_solve_triangular)/vmap()/triangular_solve | solution.py:163
  440.9 2.4 multiply_multiply_fusion.8
  446.7 40.7 %custom-call.9 = f32[8,1,64,64]{2,3,1,0:T(8,128)} custom-call(f32[8,1,64,64]{3,2,1,0:T(8,128)} %fusion.259), custom_call_target="InvertDiagBlocksLowerTriangular" | custom-call | tf_op jit(solution)/shard_map/while/body/eval_jaxpr/jit(_solve_triangular)/vmap()/triangular_solve | solution.py:163
  502.4 2.4 slice_bitcast_fusion.1
  507.0 2.9 copy.135
  509.8 55.3 %while.28 = (s32[]{:T(128)}, f32[8,64,64]{2,1,0:T(8,128)S(1)}, f32[8,64,64]{2,1,0:T(8,128)S(1)}, f32[8,64,64]{2,1,0:T(8,128)S(1)}, s32[]{:T(128)}, /*index=5*/s32[]{:T(128)}) while((s32[]{:T(128)}, f32[8,64,64]{2,1,0:T(8,128)S(1)}, f32[8,64,64]{2,1,0:T(8,128)S(1)}, f32[8,64,64]{2,1,0:T(8,128)S(1)}, s32[]{:T(128)}, ...), condition=%wide.region_9.10_spmd.clone, body=%wide.region_8.9_spmd.clone.sunk | while | flops 25296900 | bytes 917623 | solution.py:222
  510.2 3.4 collective-permute-start
  513.7 2.7 collective-permute-done
  516.8 4.4 collective-permute-start
  521.2 2.5 collective-permute-done
  524.1 4.4 collective-permute-start
  528.5 2.5 collective-permute-done
  531.4 5.2 collective-permute-start
  536.7 2.5 collective-permute-done
  539.6 5.3 collective-permute-start
  544.9 2.5 collective-permute-done
  547.8 5.3 collective-permute-start
  553.1 3.2 collective-permute-done
  556.7 5.6 collective-permute-start
  562.3 2.5 collective-permute-done
  565.1 4.1 fusion.157
  572.0 4.4 fusion.116
  578.6 4.0 convolution_convert_fusion
  585.4 23.0 %all-reduce.2 = (bf16[1,512]{1,0:T(2,128)(2,1)S(1)}, bf16[1,512]{1,0:T(2,128)(2,1)S(1)}) all-reduce(bf16[1,512]{1,0:T(2,128)(2,1)S(1)} %get-tuple-element.333, bf16[1,512]{1,0:T(2,128)(2,1)S(1)} %get-tuple-element.332), channel_id=1, replica_groups=mesh['seq'=8,'tp'=4] {'seq'}, use_global_device_ids=true, to_apply=%region_16.17 | all-reduce | flops 1024 | bytes 4096 | tf_op jit(solution)/shard_map/psum | solution.py:20
  609.0 45.8 %all-reduce.6.cloned.1.call-done = (bf16[8,64,64]{2,1,0:T(8,128)(2,1)}, bf16[8,64,64]{2,1,0:T(8,128)(2,1)}) async-done(((bf16[8,64,64]{2,1,0:T(8,128)(2,1)}, bf16[8,64,64]{2,1,0:T(8,128)(2,1)}), (bf16[8,64,64]{2,1,0:T(8,128)(2,1)}, bf16[8,64,64]{2,1,0:T(8,128)(2,1)})) %all-reduce.6.cloned.1.call-update) | async-done | bytes 131088 | tf_op jit(solution)/shard_map/psum | solution.py:20
  (348 shorter events, 169.9 us)
Async XLA Ops:
  8.0 44.3 %copy-start = (bf16[2048,512]{1,0:T(8,128)(2,1)S(1)}, bf16[2048,512]{1,0:T(8,128)(2,1)}, u32[]{:S(2)}) copy-start(bf16[2048,512]{1,0:T(8,128)(2,1)} %param.33) | copy-start | bytes 6291460
  8.0 15.7 %copy-start.11 = (bf16[384,512]{1,0:T(8,128)(2,1)S(1)}, bf16[384,512]{1,0:T(8,128)(2,1)}, u32[]{:S(2)}) copy-start(bf16[384,512]{1,0:T(8,128)(2,1)} %param.26) | copy-start | bytes 1179652
  8.0 646.8 %all-reduce.6.cloned.1.call-start = ((), (), s32[]{:S(2)}) async-start(), calls=%async_computation.2 | async-start | bytes 524288 | tf_op jit(solution)/shard_map/psum | solution.py:20
  8.1 9.7 %collective-permute-start.1 = (bf16[384,512]{1,0:T(8,128)(2,1)}, bf16[384,512]{1,0:T(8,128)(2,1)S(1)}, u32[]{:S(2)}, u32[]{:S(2)}) collective-permute-start(bf16[384,512]{1,0:T(8,128)(2,1)} %param.26), channel_id=1, source_target_pairs={{0,1},{1,2},{2,3},{3,0},{4,5},{5,6},{6,7},{7,4},{8,9},{9,10},{10,1... | collective-permute-start | bytes 1179656 | tf_op jit(solution)/shard_map/ppermute | solution.py:72
  8.6 15.2 %collective-permute-start.2 = (bf16[384,512]{1,0:T(8,128)(2,1)}, bf16[384,512]{1,0:T(8,128)(2,1)S(1)}, u32[]{:S(2)}, u32[]{:S(2)}) collective-permute-start(bf16[384,512]{1,0:T(8,128)(2,1)} %param.26), channel_id=1, source_target_pairs={{0,3},{1,0},{2,1},{3,2},{4,7},{5,4},{6,5},{7,6},{8,11},{9,8},{10,9... | collective-permute-start | bytes 1179656 | tf_op jit(solution)/shard_map/ppermute | solution.py:77
  17.7 7.3 %collective-permute-start.3 = (bf16[384,512]{1,0:T(8,128)(2,1)S(1)}, bf16[384,512]{1,0:T(8,128)(2,1)}, u32[]{:S(2)}, u32[]{:S(2)}) collective-permute-start(bf16[384,512]{1,0:T(8,128)(2,1)S(1)} %collective-permute-done.1), channel_id=1, source_target_pairs={{0,1},{1,2},{2,3},{3,0},{4,5},{5,6},{6,7},{7,4},{8,9},{9,10},{10,1... | collective-permute-start | bytes 1179656 | tf_op jit(solution)/shard_map/ppermute | solution.py:72
  23.9 3.1 copy-start.17
  26.4 9.1 %copy-start.18 = (f32[512]{0:T(512)S(1)}, f32[512]{0:T(512)}, u32[]{:S(2)}) copy-start(f32[512]{0:T(512)} %param.46) | copy-start | bytes 6148
  26.4 9.2 %copy-start.19 = (f32[512]{0:T(512)S(1)}, f32[512]{0:T(512)}, u32[]{:S(2)}) copy-start(f32[512]{0:T(512)} %param.47) | copy-start | bytes 6148
  28.7 10.6 %collective-permute-start.4 = (bf16[1,2048]{1,0:T(2,128)(2,1)S(1)}, bf16[1,2048]{1,0:T(2,128)(2,1)S(1)}, u32[]{:S(2)}, u32[]{:S(2)}) collective-permute-start(bf16[1,2048]{1,0:T(2,128)(2,1)S(1)} %slice.132), channel_id=1, source_target_pairs={{0,4},{4,8},{8,12},{12,16},{16,20},{20,24},{24,28},{1,5},{5,9},{9,... | collective-permute-start | bytes 12296 | tf_op jit(solution)/shard_map/ppermute | solution.py:15
  35.8 3.5 copy-start.21
  35.8 3.5 copy-start.22
  49.7 2.6 copy-start.23
  49.7 2.6 copy-start.24
  57.8 3.9 copy-start.25
  66.8 5.3 copy-start.15
  78.1 4.4 copy-start.9
  79.8 2.8 copy-start.7
  142.4 4.9 copy-start.1
  149.7 1.4 copy-start.2
  211.4 4.9 copy-start.1
  218.7 1.4 copy-start.2
  280.4 4.9 copy-start.1
  287.7 1.4 copy-start.2
  349.4 4.9 copy-start.1
  356.7 1.4 copy-start.2
  418.4 4.9 copy-start.1
  425.7 1.4 copy-start.2
  487.4 4.9 copy-start.1
  494.7 1.4 copy-start.2
  499.0 2.1 copy-start.3
  502.4 2.4 copy-start.6
  507.0 2.9 copy-start.4
  510.2 6.1 collective-permute-start
  516.8 6.9 %collective-permute-start = (bf16[8,64,64]{2,1,0:T(8,128)(2,1)S(1)}, bf16[8,64,64]{2,1,0:T(8,128)(2,1)S(1)}, u32[]{:S(2)}, u32[]{:S(2)}) collective-permute-start(bf16[8,64,64]{2,1,0:T(8,128)(2,1)S(1)} %fusion.267), channel_id=1, source_target_pairs={{0,4},{4,8},{8,12},{12,16},{16,20},{20,24},{24,28},{1,5},{5,9},{9,... | collective-permute-start | bytes 196616 | tf_op jit(solution)/shard_map/while/body/eval_jaxpr/ppermute | solution.py:15
  524.1 6.9 %collective-permute-start = (bf16[8,64,64]{2,1,0:T(8,128)(2,1)S(1)}, bf16[8,64,64]{2,1,0:T(8,128)(2,1)S(1)}, u32[]{:S(2)}, u32[]{:S(2)}) collective-permute-start(bf16[8,64,64]{2,1,0:T(8,128)(2,1)S(1)} %fusion.267), channel_id=1, source_target_pairs={{0,4},{4,8},{8,12},{12,16},{16,20},{20,24},{24,28},{1,5},{5,9},{9,... | collective-permute-start | bytes 196616 | tf_op jit(solution)/shard_map/while/body/eval_jaxpr/ppermute | solution.py:15
  531.4 7.7 %collective-permute-start = (bf16[8,64,64]{2,1,0:T(8,128)(2,1)S(1)}, bf16[8,64,64]{2,1,0:T(8,128)(2,1)S(1)}, u32[]{:S(2)}, u32[]{:S(2)}) collective-permute-start(bf16[8,64,64]{2,1,0:T(8,128)(2,1)S(1)} %fusion.267), channel_id=1, source_target_pairs={{0,4},{4,8},{8,12},{12,16},{16,20},{20,24},{24,28},{1,5},{5,9},{9,... | collective-permute-start | bytes 196616 | tf_op jit(solution)/shard_map/while/body/eval_jaxpr/ppermute | solution.py:15
  539.6 7.8 %collective-permute-start = (bf16[8,64,64]{2,1,0:T(8,128)(2,1)S(1)}, bf16[8,64,64]{2,1,0:T(8,128)(2,1)S(1)}, u32[]{:S(2)}, u32[]{:S(2)}) collective-permute-start(bf16[8,64,64]{2,1,0:T(8,128)(2,1)S(1)} %fusion.267), channel_id=1, source_target_pairs={{0,4},{4,8},{8,12},{12,16},{16,20},{20,24},{24,28},{1,5},{5,9},{9,... | collective-permute-start | bytes 196616 | tf_op jit(solution)/shard_map/while/body/eval_jaxpr/ppermute | solution.py:15
  547.8 8.5 %collective-permute-start = (bf16[8,64,64]{2,1,0:T(8,128)(2,1)S(1)}, bf16[8,64,64]{2,1,0:T(8,128)(2,1)S(1)}, u32[]{:S(2)}, u32[]{:S(2)}) collective-permute-start(bf16[8,64,64]{2,1,0:T(8,128)(2,1)S(1)} %fusion.267), channel_id=1, source_target_pairs={{0,4},{4,8},{8,12},{12,16},{16,20},{20,24},{24,28},{1,5},{5,9},{9,... | collective-permute-start | bytes 196616 | tf_op jit(solution)/shard_map/while/body/eval_jaxpr/ppermute | solution.py:15
  556.7 8.1 %collective-permute-start = (bf16[8,64,64]{2,1,0:T(8,128)(2,1)S(1)}, bf16[8,64,64]{2,1,0:T(8,128)(2,1)S(1)}, u32[]{:S(2)}, u32[]{:S(2)}) collective-permute-start(bf16[8,64,64]{2,1,0:T(8,128)(2,1)S(1)} %fusion.267), channel_id=1, source_target_pairs={{0,4},{4,8},{8,12},{12,16},{16,20},{20,24},{24,28},{1,5},{5,9},{9,... | collective-permute-start | bytes 196616 | tf_op jit(solution)/shard_map/while/body/eval_jaxpr/ppermute | solution.py:15
  565.1 4.3 copy-start.8
  565.1 4.3 copy-start.10
  572.0 4.5 copy-start.14
  572.0 5.5 copy-start.13
  572.0 6.6 copy-start.16
  578.6 4.1 copy-start.20
  578.6 78.0 %reduce-scatter.2.cloned.1.call-start = ((), (), s32[]{:S(2)}) async-start(), calls=%async_computation.1 | async-start | bytes 1966080 | tf_op jit(solution)/shard_map/reduce_scatter | solution.py:248
  582.6 73.9 %copy-start.12 = (bf16[384,512]{1,0:T(8,128)(2,1)S(1)}, bf16[384,512]{1,0:T(8,128)(2,1)}, u32[]{:S(2)}) copy-start(bf16[384,512]{1,0:T(8,128)(2,1)} %param.26) | copy-start | bytes 1179652
  (1 other events, 1.2 us)
Sparse Core Ops, SparseCore 0:
  578.7 76.1 all-reduce.5
Sparse Core Ops, SparseCore 1:
  582.7 33.4 reduce-scatter.1
